TPU v7x, 256 devices: a whole 4x4x8 slice. The times are simulated.
256 devices in a mesh: outer: 16 (over z, core), inner: 16 (over y, x).
Axes of the slice: x: 4, y: 4, z: 8, core: 2. Of those that a mesh axis runs over, the one named last changes fastest.
Arguments:
- queries: bfloat16 [32768, 4096], P(('outer', 'inner')), may hold values from -48 to 48
- keys: bfloat16 [32768, 1024], P(('outer', 'inner')), may hold values from -20 to 20
- values: bfloat16 [32768, 1024], P(('outer', 'inner')), may hold values from -6 to 6
- ancestors: int32 [256, 8], replicated, may hold values from -1 to 255, as said below
- token_block: int32 [32768], replicated, may hold values from 0 to 255, as said below
- positions: int32 [32768], replicated, may hold values from 0 to 1023, as said below
Outputs:
- attended: bfloat16 [32768, 4096], P(('outer', 'inner'))
Inputs may be any that keep to these rules, and one draw needn't show every extreme that they name: `ancestors`: row b lists the blocks on the path from the root block 0 to block b, root first and b last, then -1; a parent has a smaller number than its child; some row lists 8 blocks. `token_block`: each aligned span of 128 tokens belongs to one block, and every block fills exactly one span; apart from block 0, no two blocks of one root path lie in the same aligned group of 2048 tokens. `positions`: a token's position is 128 times (the number of blocks on its block's root path minus 1) plus its offset within its span.
All inputs are finite; a program needn't handle non-finite values.
Results may differ from a plain program's by a relative error of at most 0.0065.
Values may be sent and summed in bfloat16 or wider, within the bound.
No kernel may reach another device: no remote copies, remote signals or barrier semaphores. Data moves between devices by JAX's collectives and lax.ppermute only.
A program may use at most 128 MiB of HBM per device.

v0:
```python
import jax
import jax.numpy as jnp
from jax import lax
from jax.sharding import PartitionSpec as P

HEADS = 32
KV_HEADS = 8
HEAD_DIM = 128
BLOCK = 128
ANC_MAX = 8


ROTARY_BASE = 500000.0


def rotate(matrix, places, head_count):
    row_count = matrix.shape[0]
    head_width = matrix.shape[1] // head_count
    half_width = head_width // 2
    inverse = ROTARY_BASE ** (-2.0 * jnp.arange(half_width, dtype=jnp.float32) / head_width)
    angles = places.astype(jnp.float32)[:, None] * inverse[None, :]
    cosine = jnp.cos(angles)[:, None, :]
    sine_part = jnp.sin(angles)[:, None, :]
    unfolded = matrix.astype(jnp.float32).reshape(row_count, head_count, head_width)
    leading = unfolded[:, :, :half_width]
    trailing = unfolded[:, :, half_width:]
    turned = jnp.concatenate(
        [leading * cosine - trailing * sine_part, trailing * cosine + leading * sine_part], axis=2
    )
    return turned.reshape(row_count, head_count * head_width).astype(jnp.bfloat16)


def shards(queries, keys, values, ancestors, token_block, positions):
    tok_rows = queries.shape[0]
    span_count = tok_rows // BLOCK
    group_size = HEADS // KV_HEADS
    kv_width = keys.shape[1]
    outer_count = lax.axis_size("outer")
    inner_count = lax.axis_size("inner")
    outer_me = lax.axis_index("outer")
    inner_me = lax.axis_index("inner")
    device_me = outer_me * inner_count + inner_me
    start_row = device_me * tok_rows
    own_places = lax.dynamic_slice_in_dim(positions, start_row, tok_rows)
    rot_q = rotate(queries, own_places, HEADS)
    rot_k = rotate(keys, own_places, KV_HEADS)
    block_count = ancestors.shape[0]
    block_ids = jnp.arange(block_count, dtype=jnp.int32)
    span_blocks = token_block[::BLOCK]
    span_of = jnp.sum(
        jnp.where(span_blocks[:, None] == block_ids[None, :], block_ids[:, None], 0), axis=0
    )
    group_spans = inner_count * span_count
    capacity = 2
    span_ids = jnp.arange(span_count, dtype=jnp.int32)
    slot_ids = jnp.arange(capacity, dtype=jnp.int32)
    bundled = (
        lax.all_gather(rot_k, "inner", axis=0, tiled=True),
        lax.all_gather(values, "inner", axis=0, tiled=True),
    )
    key_blocks = bundled[0].reshape(group_spans, BLOCK, kv_width)
    value_blocks = bundled[1].reshape(group_spans, BLOCK, kv_width)
    dest_outer = jnp.arange(outer_count, dtype=jnp.int32)
    dest_spans = (dest_outer[:, None] * inner_count + inner_me) * span_count + span_ids[None, :]
    dest_lineage = ancestors[span_blocks[dest_spans]]
    lineage_spans = span_of[jnp.maximum(dest_lineage, 0)]
    counted = dest_lineage >= 0
    matches = counted & (lineage_spans // group_spans == outer_me)
    slot_rank = jnp.cumsum(matches.astype(jnp.int32), axis=2) - 1
    local_spans = lineage_spans - outer_me * group_spans
    picked = jnp.sum(
        jnp.where(
            matches[..., None] & (slot_rank[..., None] == slot_ids), local_spans[..., None], 0
        ),
        axis=2,
    )
    send_keys = key_blocks[picked]
    send_values = value_blocks[picked]
    received = (
        lax.all_to_all(send_keys, "outer", split_axis=0, concat_axis=0, tiled=True),
        lax.all_to_all(send_values, "outer", split_axis=0, concat_axis=0, tiled=True),
    )
    own_spans = device_me * span_count + span_ids
    own_lineage = ancestors[span_blocks[own_spans]]
    own_valid = own_lineage >= 0
    own_span_of = span_of[jnp.maximum(own_lineage, 0)]
    own_groups = own_span_of // group_spans
    path_ids = jnp.arange(ANC_MAX, dtype=jnp.int32)
    earlier = path_ids[None, :] < path_ids[:, None]
    same_group = (
        own_valid[:, None, :]
        & (own_groups[:, :, None] == own_groups[:, None, :])
        & earlier[None, :, :]
    )
    own_rank = jnp.minimum(jnp.sum(same_group.astype(jnp.int32), axis=2), capacity - 1)
    slot_index = (own_groups * span_count + span_ids[:, None]) * capacity + own_rank
    slot_total = outer_count * span_count * capacity
    got_keys = received[0].reshape(slot_total, BLOCK, kv_width)[slot_index]
    got_values = received[1].reshape(slot_total, BLOCK, kv_width)[slot_index]
    offsets = jnp.arange(BLOCK, dtype=jnp.int32)
    key_index = (own_span_of[:, :, None] * BLOCK + offsets[None, None, :]).reshape(
        span_count, ANC_MAX * BLOCK
    )
    key_places = positions[key_index]
    query_places = own_places.reshape(span_count, BLOCK)
    allowed = jnp.repeat(own_valid, BLOCK, axis=1)[:, None, :] & (
        key_places[:, None, :] <= query_places[:, :, None]
    )
    query_rows = rot_q.reshape(span_count, BLOCK, KV_HEADS, group_size, HEAD_DIM)
    key_rows = got_keys.reshape(span_count, ANC_MAX * BLOCK, KV_HEADS, HEAD_DIM)
    value_rows = got_values.reshape(span_count, ANC_MAX * BLOCK, KV_HEADS, HEAD_DIM)
    scaling = HEAD_DIM ** (-0.5)
    scores = (
        jnp.einsum("rtkgd,rukd->rtkgu", query_rows, key_rows, preferred_element_type=jnp.float32)
        * scaling
    )
    wide_mask = allowed[:, :, None, None, :]
    top_score = jnp.max(jnp.where(wide_mask, scores, -jnp.inf), axis=4)
    weights = jnp.where(wide_mask, jnp.exp(scores - top_score[..., None]), 0.0)
    totals = jnp.sum(weights, axis=4)
    mixed_sum = jnp.einsum(
        "rtkgu,rukd->rtkgd",
        weights.astype(jnp.bfloat16),
        value_rows,
        preferred_element_type=jnp.float32,
    )
    attended = (
        (mixed_sum / totals[..., None]).reshape(tok_rows, HEADS * HEAD_DIM).astype(jnp.bfloat16)
    )
    return attended


def solution(mesh):
    placed = (
        P(("outer", "inner"), None),
        P(("outer", "inner"), None),
        P(("outer", "inner"), None),
        P(),
        P(),
        P(),
    )
    return jax.shard_map(
        shards, mesh=mesh, in_specs=placed, out_specs=P(("outer", "inner"), None), check_vma=False
    )
```

profile of v0, /device:TPU:1, one launch (start us, length us, event | category | flops | bytes accessed | tf_op | source)
XLA Modules:
  0.0 498.6 jit_solution(17158688067835165841)
XLA Ops:
  6.5 0.0 copy-start.3
  6.5 0.0 all-gather.5.cloned.1.call-start
  6.6 1.0 convert_bitcast_fusion.1
  7.6 0.1 copy.50
  7.7 0.8 fusion.28
  8.4 0.3 multiply_cosine_fusion
  8.7 0.3 subtract_convert_fusion.1
  9.0 0.1 pad_maximum_fusion.1
  9.2 0.8 copy.67
  10.0 0.0 all-gather.5.cloned.1.call-update
  10.0 1.1 slice.15
  11.1 0.0 copy-done.3
  11.1 0.1 copy.29
  11.3 0.7 gather_fusion
  11.9 0.6 gather_fusion.1
  12.5 0.1 reshape.866
  12.6 0.1 select_reduce_fusion
  12.7 1.3 gather_fusion.2
  14.0 0.1 gather.45
  14.1 0.1 copy.32
  14.2 0.2 reduce_window_sum.11
  14.4 0.1 copy.31
  14.4 0.1 copy.30
  14.6 0.1 copy.33
  14.6 0.1 reshape.874
  14.7 55.4 %all-gather.5.cloned.1.call-done = bf16[2048,1024]{1,0:T(8,128)(2,1)} async-done(((bf16[128,1024]{1,0:T(8,128)(2,1)}), bf16[2048,1024]{1,0:T(8,128)(2,1)}) %all-gather.5.cloned.1.call-update) | async-done | bytes 4194320 | tf_op jit(solution)/shard_map/all_gather | solution.py:58
  70.2 6.9 %gather_fusion.7 = bf16[32,128,1024]{2,1,0:T(8,128)(2,1)} fusion(bf16[16,128,1024]{2,1,0:T(8,128)(2,1)} %bitcast.102, s32[1024]{0:T(1024)S(1)} %pad_clamp_fusion.2), kind=kCustom, calls=%fused_computation.7 | custom fusion | bytes 16777344 | tf_op jit(solution)/shard_map/gather | solution.py:77
  77.1 7.8 %all-to-all-start.1 = ((bf16[16,1,2,128,1024]{4,3,2,1,0:T(8,128)(2,1)}), bf16[16,1,2,128,1024]{4,3,2,1,0:T(8,128)(2,1)}, u32[]{:S(2)}, u32[]{:S(2)}) async-start(bf16[16,1,2,128,1024]{4,3,2,1,0:T(8,128)(2,1)} %bitcast.100), calls=%async_computation.1 | async-start | bytes 16777216 | tf_op jit(solution)/shard_map/all_to_all | solution.py:80
  85.0 0.0 all-gather.3.cloned.1.call-start
  85.0 0.7 all-gather.3.cloned.1.call-update
  85.7 58.0 %all-gather.3.cloned.1.call-done = bf16[2048,1024]{1,0:T(8,128)(2,1)} async-done(((bf16[128,1024]{1,0:T(8,128)(2,1)}), bf16[2048,1024]{1,0:T(8,128)(2,1)}) %all-gather.3.cloned.1.call-update) | async-done | bytes 4194320 | tf_op jit(solution)/shard_map/all_gather | solution.py:59
  143.7 6.9 %gather_fusion.3 = bf16[32,128,1024]{2,1,0:T(8,128)(2,1)} fusion(bf16[16,128,1024]{2,1,0:T(8,128)(2,1)} %bitcast.103, s32[1024]{0:T(1024)S(1)} %pad_clamp_fusion.2), kind=kCustom, calls=%fused_computation.3 | custom fusion | bytes 16777344 | tf_op jit(solution)/shard_map/gather | solution.py:78
  150.6 117.7 %all-to-all-done.1 = bf16[16,1,2,128,1024]{4,3,2,1,0:T(8,128)(2,1)} async-done(((bf16[16,1,2,128,1024]{4,3,2,1,0:T(8,128)(2,1)}), bf16[16,1,2,128,1024]{4,3,2,1,0:T(8,128)(2,1)}, u32[]{:S(2)}, u32[]{:S(2)}) %all-to-all-start.1) | async-done | bytes 8388640 | tf_op jit(solution)/shard_map/all_to_all | solution.py:80
  268.4 0.0 copy-start
  268.4 5.7 %all-to-all-start = ((bf16[16,1,2,128,1024]{4,3,2,1,0:T(8,128)(2,1)}), bf16[16,1,2,128,1024]{4,3,2,1,0:T(8,128)(2,1)}, u32[]{:S(2)}, u32[]{:S(2)}) async-start(bf16[16,1,2,128,1024]{4,3,2,1,0:T(8,128)(2,1)} %bitcast.99), calls=%async_computation | async-start | bytes 16777216 | tf_op jit(solution)/shard_map/all_to_all | solution.py:81
  274.1 0.0 copy-start.2
  274.1 0.6 dynamic-slice.5
  276.6 0.2 maximum_reduce_fusion
  276.8 0.6 gather_fusion.4
  277.4 0.1 compare_select_fusion
  277.5 0.0 copy-done
  277.5 6.2 %gather_fusion.6 = s32[1024]{0:T(1024)S(1)} fusion(s32[32768]{0:T(1024)S(1)} %copy-done, s32[1024]{0:T(1024)S(1)} %broadcast_clamp_fusion), kind=kCustom, calls=%fused_computation.6 | custom fusion | bytes 12288 | tf_op jit(solution)/shard_map/gather | solution.py:104
  283.7 0.0 copy-done.2
  283.7 0.2 convert_bitcast_fusion
  283.9 0.4 copy.53
  284.3 0.2 compare_reduce_fusion
  284.5 0.2 convert_reduce_fusion
  284.7 0.7 fusion.29
  285.4 2.5 subtract_convert_fusion
  287.9 0.6 pad_maximum_fusion
  288.5 0.1 broadcast_bitcast_fusion
  288.6 0.3 compare_and_fusion
  288.9 5.5 %gather_fusion.8 = bf16[8,128,1024]{2,1,0:T(8,128)(2,1)} fusion(bf16[32,128,1024]{2,1,0:T(8,128)(2,1)} %bitcast.20, s32[1024]{0:T(1024)S(1)} %pad_clamp_fusion), kind=kCustom, calls=%fused_computation.8 | custom fusion | bytes 4194336 | tf_op jit(solution)/shard_map/gather | solution.py:98
  294.4 2.2 copy.52
  296.6 160.9 %all-to-all-done = bf16[16,1,2,128,1024]{4,3,2,1,0:T(8,128)(2,1)} async-done(((bf16[16,1,2,128,1024]{4,3,2,1,0:T(8,128)(2,1)}), bf16[16,1,2,128,1024]{4,3,2,1,0:T(8,128)(2,1)}, u32[]{:S(2)}, u32[]{:S(2)}) %all-to-all-start) | async-done | bytes 8388640 | tf_op jit(solution)/shard_map/all_to_all | solution.py:81
  457.5 5.4 %gather_fusion.5 = bf16[8,128,1024]{2,1,0:T(8,128)(2,1)} fusion(bf16[32,128,1024]{2,1,0:T(8,128)(2,1)} %bitcast.6, s32[1024]{0:T(1024)S(1)} %pad_clamp_fusion), kind=kCustom, calls=%fused_computation.5 | custom fusion | bytes 4194336 | tf_op jit(solution)/shard_map/gather | solution.py:99
  462.9 3.6 copy.49
  466.5 7.0 %fusion = (f32[128,8,4]{0,2,1:T(4,128)S(1)}, f32[8,1024,128,4]{2,1,3,0:T(8,128)}) fusion(pred[128,1024]{0,1:T(8,128)(4,1)S(1)} %compare_and_fusion, bf16[128,8,4,128]{3,0,2,1:T(8,128)(2,1)S(1)} %bitcast.107, bf16[1024,8,128,1]{2,1,0,3:T(8,128)(2,1)S(1)} %bitcast.104), kind=kOutput, calls=%fused_computation.11 | convolution fusion | flops 1086320640 | bytes 20070400 | tf_op jit(solution)/shard_map/rtkgd,rukd->rtkgu/dot_general | solution.py:114
  473.5 0.0 copy-start.1
  473.5 9.3 %fusion.3 = f32[128,8,4]{0,2,1:T(4,128)S(1)} fusion(f32[8,1024,128,4]{2,1,3,0:T(8,128)} %get-tuple-element.42, f32[128,8,4]{0,2,1:T(4,128)S(1)} %get-tuple-element.41, pred[128,1024]{0,1:T(8,128)(4,1)S(1)} %compare_and_fusion), kind=kLoop, calls=%fused_computation.14 | loop fusion | flops 16773120 | bytes 16941056 | tf_op jit(solution)/shard_map/reduce_sum | solution.py:120
  482.8 0.0 copy-done.1
  482.8 7.7 %fusion.9 = bf16[1,128,8,4,128]{1,4,3,2,0:T(8,128)(2,1)S(1)} fusion(f32[128,8,4]{0,2,1:T(4,128)S(1)} %fusion.3, f32[8,1024,128,4]{2,1,3,0:T(8,128)} %get-tuple-element.42, f32[128,8,4]{0,2,1:T(4,128)S(1)} %get-tuple-element.41, pred[128,1024]{0,1:T(8,128)(4,1)S(1)} %compare_and_fusion, bf16[1024,8,128,1]{2,1,0,3:T(8,128)(2,1)S(1)} %bitcast.109), kind=kOutput, calls=%fused_computation.20 | convolution fusion | flops 1091567616 | bytes 20086784 | tf_op jit(solution)/shard_map/rtkgu,rukd->rtkgd/dot_general | solution.py:121
  490.5 1.3 copy.39
  (19 shorter events, 0.2 us)
Async XLA Ops:
  6.5 4.6 copy-start.3
  6.5 63.6 %all-gather.5.cloned.1.call-start = ((), (), s32[]{:S(2)}) async-start(), calls=%async_computation.3 | async-start | bytes 4456448 | tf_op jit(solution)/shard_map/all_gather | solution.py:58
  77.1 191.2 %all-to-all-start.1 = ((bf16[16,1,2,128,1024]{4,3,2,1,0:T(8,128)(2,1)}), bf16[16,1,2,128,1024]{4,3,2,1,0:T(8,128)(2,1)}, u32[]{:S(2)}, u32[]{:S(2)}) async-start(bf16[16,1,2,128,1024]{4,3,2,1,0:T(8,128)(2,1)} %bitcast.100), calls=%async_computation.1 | async-start | bytes 16777216 | tf_op jit(solution)/shard_map/all_to_all | solution.py:80
  85.0 58.7 %all-gather.3.cloned.1.call-start = ((), (), s32[]{:S(2)}) async-start(), calls=%async_computation.2 | async-start | bytes 4456448 | tf_op jit(solution)/shard_map/all_gather | solution.py:59
  268.4 9.2 %copy-start = (s32[32768]{0:T(1024)S(1)}, s32[32768]{0:T(1024)}, u32[]{:S(2)}) copy-start(s32[32768]{0:T(1024)} %param.11) | copy-start | bytes 393220
  268.4 189.1 %all-to-all-start = ((bf16[16,1,2,128,1024]{4,3,2,1,0:T(8,128)(2,1)}), bf16[16,1,2,128,1024]{4,3,2,1,0:T(8,128)(2,1)}, u32[]{:S(2)}, u32[]{:S(2)}) async-start(bf16[16,1,2,128,1024]{4,3,2,1,0:T(8,128)(2,1)} %bitcast.99), calls=%async_computation | async-start | bytes 16777216 | tf_op jit(solution)/shard_map/all_to_all | solution.py:81
  274.1 9.6 %copy-start.2 = (bf16[128,4096]{1,0:T(8,128)(2,1)S(1)}, bf16[128,4096]{1,0:T(8,128)(2,1)}, u32[]{:S(2)}) copy-start(bf16[128,4096]{1,0:T(8,128)(2,1)} %param.6) | copy-start | bytes 3145732
  473.5 9.3 %copy-start.1 = (bf16[128,8,8,128]{3,2,1,0:T(8,128)(2,1)S(1)}, bf16[128,8,8,128]{3,2,1,0:T(8,128)(2,1)}, u32[]{:S(2)}) copy-start(bf16[128,8,8,128]{3,2,1,0:T(8,128)(2,1)} %copy.49) | copy-start | bytes 6291460
Sparse Core Ops, SparseCore 0:
  10.1 60.0 all-gather.4
  88.2 55.4 all-gather.2
where the time goes:
time: 499 us
  waiting for transfers between devices  393 us (79%)
  local copies, waits for them, and re-layouts  45.6 us (9%)
  other arithmetic  16.5 us (3%)
  between operations  15.5 us (3%)
  matrix products  14.7 us (3%)
  starting transfers between devices  13.6 us (3%)
    all_to_all x1, waiting for transfers between devices, shards(): lax.all_to_all(send_values, 'outer', split_axis=0, concat_axis=0, tiled=T...  161 us
    all_to_all x1, waiting for transfers between devices, shards(): lax.all_to_all(send_keys, 'outer', split_axis=0, concat_axis=0, tiled=True)  118 us
    all_gather x1, waiting for transfers between devices, shards(): lax.all_gather(values, 'inner', axis=0, tiled=True)  58 us
    all_gather x1, waiting for transfers between devices, shards(): lax.all_gather(rot_k, 'inner', axis=0, tiled=True)  55.4 us
  transfers between devices with their start and end apart: 4, of which 4 were waited for; matrix products, arithmetic and copies ran while one was open for 6% of the time, Pallas kernels for 0%

commit v1 on v0

v1 whole, which is shorter than its diff:
```python
import functools

import jax
import jax.numpy as jnp
import numpy as np
from jax import lax
from jax.experimental import pallas as pl
from jax.experimental.pallas import tpu as pltpu
from jax.sharding import Mesh
from jax.sharding import PartitionSpec as P

HEADS = 32
KV_HEADS = 8
GROUP = HEADS // KV_HEADS
HEAD_DIM = 128
BLOCK = 128
ANC_MAX = 8
SLOTS = ANC_MAX - 1
DEVICES = 256
ROTARY_BASE = 500000.0
ALL_AXES = ("z", "c", "i")
NEG = -1e30
EXP2_SCALE = float(HEAD_DIM**-0.5 * np.log2(np.e))


def inverse_row():
    half = HEAD_DIM // 2
    inv = (ROTARY_BASE ** (-2.0 * np.arange(half, dtype=np.float64) / HEAD_DIM)).astype(np.float32)
    return np.concatenate([inv, inv])[None, :]


def turn(x, cosine, sine):
    return (x * cosine + pltpu.roll(x, HEAD_DIM // 2, 1) * sine).astype(jnp.bfloat16)


def spread_kernel(base_ref, inv_ref, k_ref, v_ref, send_ref, cos_ref, sin_ref, own_ref):
    rows = lax.broadcasted_iota(jnp.int32, (BLOCK, HEAD_DIM), 0) + base_ref[0]
    lanes = lax.broadcasted_iota(jnp.int32, (BLOCK, HEAD_DIM), 1)
    angles = rows.astype(jnp.float32) * inv_ref[...]
    cosine = jnp.cos(angles)
    sine = jnp.sin(angles)
    sine = jnp.where(lanes < HEAD_DIM // 2, -sine, sine)
    cos_ref[...] = cosine
    sin_ref[...] = sine
    for h in range(KV_HEADS):
        cols = slice(h * HEAD_DIM, (h + 1) * HEAD_DIM)
        turned = turn(k_ref[:, cols].astype(jnp.float32), cosine, sine)
        own_ref[:, cols] = turned
        plain = v_ref[:, cols]
        for high in range(2):
            for low in range(8):
                t = (high * 8 + low) * 8
                send_ref[low, h, 0, high] = turned[t : t + 8]
                send_ref[low, h, 1, high] = plain[t : t + 8]


def pick_kernel(count, idx_ref, src_ref, out_ref):
    def one(d, carry):
        for j in range(count):
            out_ref[d, j] = src_ref[idx_ref[d * count + j]]
        return carry

    lax.fori_loop(0, out_ref.shape[0], one, 0)


def attend_kernel(alive_ref, cos_ref, sin_ref, q_ref, ko_ref, vo_ref, ka_ref, va_ref, out_ref):
    cosine = cos_ref[...]
    sine = sin_ref[...]
    parts = [
        turn(q_ref[:, g * HEAD_DIM : (g + 1) * HEAD_DIM].astype(jnp.float32), cosine, sine)
        for g in range(GROUP)
    ]
    q = jnp.concatenate(parts, axis=0)
    dims = (((1,), (1,)), ((), ()))
    far = lax.dot_general(q, ka_ref[...], dims, preferred_element_type=jnp.float32)
    near = lax.dot_general(q, ko_ref[...], dims, preferred_element_type=jnp.float32)
    keys = ka_ref.shape[0]
    column = lax.broadcasted_iota(jnp.int32, (1, keys), 1)
    slot = (column // 64) % SLOTS
    far = far + jnp.where(slot < alive_ref[0], 0.0, NEG)
    row = lax.broadcasted_iota(jnp.int32, near.shape, 0) % BLOCK
    col = lax.broadcasted_iota(jnp.int32, near.shape, 1)
    near = jnp.where(col <= row, near, NEG)
    top = jnp.maximum(
        jnp.max(far, axis=1, keepdims=True), jnp.max(near, axis=1, keepdims=True)
    )
    far_w = jnp.exp2((far - top) * EXP2_SCALE)
    near_w = jnp.exp2((near - top) * EXP2_SCALE)
    total = jnp.sum(far_w, axis=1, keepdims=True) + jnp.sum(near_w, axis=1, keepdims=True)
    mixed = jnp.dot(far_w.astype(jnp.bfloat16), va_ref[...], preferred_element_type=jnp.float32)
    mixed += jnp.dot(near_w.astype(jnp.bfloat16), vo_ref[...], preferred_element_type=jnp.float32)
    done = (mixed / total).astype(jnp.bfloat16)
    for g in range(GROUP):
        out_ref[:, g * HEAD_DIM : (g + 1) * HEAD_DIM] = done[g * BLOCK : (g + 1) * BLOCK]


SMEM = pl.BlockSpec(memory_space=pltpu.SMEM)


def shards(queries, keys, values, ancestors, token_block, positions):
    bf = jnp.bfloat16
    me = lax.axis_index(ALL_AXES)
    base = lax.dynamic_slice_in_dim(positions, me * BLOCK, 1)
    span_blocks = token_block.reshape(DEVICES, BLOCK)[:, 0]
    ids = jnp.arange(DEVICES, dtype=jnp.int32)
    span_of = jnp.sum(jnp.where(span_blocks[:, None] == ids[None, :], ids[:, None], 0), axis=0)
    lineage = ancestors[span_blocks]
    depth = jnp.sum((lineage >= 0).astype(jnp.int32), axis=1)
    spans = span_of[jnp.maximum(lineage, 0)][:, :SLOTS]
    alive = lax.dynamic_slice_in_dim(depth - 1, me, 1)

    send, cosine, sine, own_k = pl.pallas_call(
        spread_kernel,
        out_shape=(
            jax.ShapeDtypeStruct((8, KV_HEADS, 2, 2, 8, HEAD_DIM), bf),
            jax.ShapeDtypeStruct((BLOCK, HEAD_DIM), jnp.float32),
            jax.ShapeDtypeStruct((BLOCK, HEAD_DIM), jnp.float32),
            jax.ShapeDtypeStruct((BLOCK, KV_HEADS * HEAD_DIM), bf),
        ),
        in_specs=[SMEM] + [pl.BlockSpec(memory_space=pltpu.VMEM)] * 3,
    )(base, jnp.asarray(inverse_row()), keys, values)
    chunks = lax.all_to_all(
        send.reshape(DEVICES, 8, HEAD_DIM), ALL_AXES, 0, 0, tiled=True
    )
    packed = pl.pallas_call(
        functools.partial(pick_kernel, SLOTS),
        out_shape=jax.ShapeDtypeStruct((DEVICES, SLOTS, 8, HEAD_DIM), bf),
        in_specs=[SMEM, pl.BlockSpec(memory_space=pltpu.VMEM)],
    )(spans.reshape(-1), chunks)
    got = lax.all_to_all(
        packed.reshape(DEVICES, SLOTS * 8, HEAD_DIM), ALL_AXES, 0, 0, tiled=True
    )
    got = got.reshape(8, KV_HEADS, 2, 2, SLOTS, 8, HEAD_DIM).transpose(2, 1, 3, 4, 0, 5, 6)
    got = got.reshape(2, KV_HEADS, SLOTS * BLOCK, HEAD_DIM)
    return attend(alive, cosine, sine, queries, own_k, values, got)


def attend(alive, cosine, sine, queries, own_k, values, got):
    table = pl.BlockSpec((BLOCK, HEAD_DIM), lambda h: (0, 0))
    head = pl.BlockSpec((BLOCK, HEAD_DIM), lambda h: (0, h))
    heads = pl.BlockSpec((BLOCK, GROUP * HEAD_DIM), lambda h: (0, h))
    far_k = pl.BlockSpec((None, None, SLOTS * BLOCK, HEAD_DIM), lambda h: (0, h, 0, 0))
    far_v = pl.BlockSpec((None, None, SLOTS * BLOCK, HEAD_DIM), lambda h: (1, h, 0, 0))
    return pl.pallas_call(
        attend_kernel,
        grid=(KV_HEADS,),
        out_shape=jax.ShapeDtypeStruct(queries.shape, jnp.bfloat16),
        in_specs=[SMEM, table, table, heads, head, head, far_k, far_v],
        out_specs=heads,
    )(alive, cosine, sine, queries, own_k, values, got, got)


def solution(mesh):
    fine = Mesh(mesh.devices.reshape(8, 2, 16), ALL_AXES)
    rows = P(ALL_AXES, None)
    return jax.shard_map(
        shards,
        mesh=fine,
        in_specs=(rows, rows, rows, P(), P(), P()),
        out_specs=rows,
        check_vma=False,
    )
```

time: 499 us -> 161 us (0.32)
  waiting for transfers between devices: 393 us -> 87.8 us
  local copies, waits for them, and re-layouts: 45.6 us -> 23.4 us
  Pallas kernels: 0 us -> 21.9 us
  between operations: 15.5 us -> 0.08 us
  other arithmetic: 16.5 us -> 1.29 us
  matrix products: 14.7 us -> 0 us
  starting transfers between devices: 13.6 us -> 26.4 us
    all_to_all x2, waiting for transfers between devices: 279 us -> 87.8 us  [the longest x1 84 us: shards(): lax.all_to_all(packed.reshape(DEVICES, SLOTS * 8, HEAD_DIM), ALL_AXES, 0,...]
    all_gather x2 -> x0, waiting for transfers between devices: 113 us -> none  [the longest x1 58 us: shards(): lax.all_gather(values, 'inner', axis=0, tiled=True)]
    pallas_call x0 -> x3, Pallas kernels: none -> 21.9 us  [the longest x1 12.7 us: attend(): pl.pallas_call(attend_kernel, grid=(KV_HEADS,), out_shape=jax.ShapeDtypeS...]
    gather x11 -> x3, local copies, waits for them, and re-layouts: 34.7 us -> 14 us  [the longest x2 13.2 us: shards(): spans = span_of[jnp.maximum(lineage, 0)][:, :SLOTS]]
    dot_general x2 -> x0, matrix products: 14.7 us -> none  [the longest x1 7.67 us: shards(): jnp.einsum('rtkgu,rukd->rtkgd', weights.astype(jnp.bfloat16), value_rows,...]
    all_to_all x2, starting transfers between devices: 13.6 us -> 26.4 us  [the longest x1 15.6 us: shards(): lax.all_to_all(send.reshape(DEVICES, 8, HEAD_DIM), ALL_AXES, 0, 0, tiled=...]
    reduce_sum x4 -> x1, other arithmetic: 9.58 us -> 0.12 us  [shards(): jnp.sum(jnp.where(span_blocks[:, None] == ids[None, :], ids[:, None], 0),...]
    unnamed x14 -> x3, local copies, waits for them, and re-layouts: 7.13 us -> 1.61 us
  transfers between devices with their start and end apart: 4 -> 2, of which waited for: 4 -> 2; matrix products, arithmetic and copies ran while one was open for 6% -> 11% of each run, Pallas kernels for 0% -> 0%
where the time goes in v1:
time: 161 us
  waiting for transfers between devices  87.8 us (55%)
  starting transfers between devices  26.4 us (16%)
  local copies, waits for them, and re-layouts  23.4 us (15%)
  Pallas kernels  21.9 us (14%)
    all_to_all x1, waiting for transfers between devices, shards(): lax.all_to_all(packed.reshape(DEVICES, SLOTS * 8, HEAD_DIM), ALL_AXES, 0,...  84 us
    all_to_all x1, starting transfers between devices, shards(): lax.all_to_all(send.reshape(DEVICES, 8, HEAD_DIM), ALL_AXES, 0, 0, tiled=...  15.6 us
    gather x2, local copies, waits for them, and re-layouts, shards(): spans = span_of[jnp.maximum(lineage, 0)][:, :SLOTS]  13.2 us
    pallas_call x1, Pallas kernels, attend(): pl.pallas_call(attend_kernel, grid=(KV_HEADS,), out_shape=jax.ShapeDtypeS...  12.7 us
    all_to_all x1, starting transfers between devices, shards(): lax.all_to_all(packed.reshape(DEVICES, SLOTS * 8, HEAD_DIM), ALL_AXES, 0,...  10.8 us
    pallas_call x1, Pallas kernels, shards(): pl.pallas_call(functools.partial(pick_kernel, SLOTS), out_shape=jax.Shape...  6.21 us
    transpose x1, local copies, waits for them, and re-layouts, shards(): got.reshape(8, KV_HEADS, 2, 2, SLOTS, 8, HEAD_DIM)  4.9 us
    all_to_all x1, waiting for transfers between devices, shards(): lax.all_to_all(send.reshape(DEVICES, 8, HEAD_DIM), ALL_AXES, 0, 0, tiled=...  3.79 us
  transfers between devices with their start and end apart: 2, of which 2 were waited for; matrix products, arithmetic and copies ran while one was open for 11% of the time, Pallas kernels for 0%

profile of v1, /device:TPU:1, one launch (start us, length us, event | category | flops | bytes accessed | tf_op | source)
XLA Modules:
  0.0 161.0 jit_solution(16197722192015578871)
XLA Ops:
  0.0 1.3 dynamic_slice.7.base_ref
  1.3 3.0 %shard_map.73 = (bf16[8,8,2,2,8,128]{5,4,3,2,1,0:T(8,128)(2,1)}, f32[128,128]{1,0:T(8,128)}, f32[128,128]{1,0:T(8,128)}, bf16[128,1024]{1,0:T(8,128)(2,1)}) custom-call(s32[1]{0:T(128)} %dynamic_slice.7.base_ref, f32[1,128]{1,0:T(1,128)} %constant.37.clone.inv_ref, bf16[128,1024]{1,0:T(8,128)(2,1)} %k_ref.1, bf16[128,1024]{1,0:T(8,128)(2,1)} %vo_ref.1), custom_call_target="tpu_custom_call" | custom-call | tf_op jit(solution)/shard_map/pallas_call | solution.py:112
  4.4 15.6 %all-to-all-start = ((bf16[256,8,128]{2,1,0:T(8,128)(2,1)}), bf16[256,8,128]{2,1,0:T(8,128)(2,1)S(1)}, u32[]{:S(2)}, u32[]{:S(2)}) async-start(bf16[256,8,128]{2,1,0:T(8,128)(2,1)} %bitcast.11), calls=%async_computation | async-start | bytes 1048576 | tf_op jit(solution)/shard_map/all_to_all | solution.py:122
  20.0 0.8 copy.13
  20.9 1.0 slice_reduce_fusion
  21.9 0.7 gather_fusion
  22.7 0.1 broadcast_maximum_fusion
  22.8 0.1 reshape.43
  22.9 0.1 select_reduce_fusion
  23.0 13.1 %gather_fusion.1 = s32[2048]{0:T(1024)S(1)} fusion(s32[256]{0:T(256)S(1)} %select_reduce_fusion, s32[2048]{0:T(1024)S(1)} %broadcast_clamp_fusion), kind=kCustom, calls=%fused_computation.1 | custom fusion | bytes 24576 | tf_op jit(solution)/shard_map/gather | solution.py:109
  36.2 0.1 reshape.42
  36.3 0.8 reshape.28.idx_ref
  37.1 3.8 %all-to-all-done.src_ref = bf16[256,8,128]{2,1,0:T(8,128)(2,1)S(1)} async-done(((bf16[256,8,128]{2,1,0:T(8,128)(2,1)}), bf16[256,8,128]{2,1,0:T(8,128)(2,1)S(1)}, u32[]{:S(2)}, u32[]{:S(2)}) %all-to-all-start) | async-done | bytes 524320 | tf_op jit(solution)/shard_map/all_to_all | solution.py:122
  40.9 0.0 copy-start
  40.9 0.8 copy-done
  41.7 6.2 %shard_map.74 = bf16[256,7,8,128]{3,2,1,0:T(8,128)(2,1)} custom-call(s32[1792]{0:T(1024)} %reshape.28.idx_ref, bf16[256,8,128]{2,1,0:T(8,128)(2,1)} %copy-done), custom_call_target="tpu_custom_call" | custom-call | tf_op jit(solution)/shard_map/pallas_call | solution.py:125
  47.9 10.8 %all-to-all-start.1 = ((bf16[256,56,128]{2,1,0:T(8,128)(2,1)}), bf16[256,56,128]{2,1,0:T(8,128)(2,1)}, u32[]{:S(2)}, u32[]{:S(2)}) async-start(bf16[256,56,128]{2,1,0:T(8,128)(2,1)} %bitcast.10), calls=%async_computation.1 | async-start | bytes 7340032 | tf_op jit(solution)/shard_map/all_to_all | solution.py:130
  58.7 0.7 dynamic_slice.6.alive_ref
  59.4 84.0 %all-to-all-done.1 = bf16[256,56,128]{2,1,0:T(8,128)(2,1)} async-done(((bf16[256,56,128]{2,1,0:T(8,128)(2,1)}), bf16[256,56,128]{2,1,0:T(8,128)(2,1)}, u32[]{:S(2)}, u32[]{:S(2)}) %all-to-all-start.1) | async-done | bytes 3670048 | tf_op jit(solution)/shard_map/all_to_all | solution.py:130
  143.4 4.9 %copy.14 = bf16[2,8,2,7,8,8,128]{6,5,4,3,2,1,0:T(8,128)(2,1)} copy(bf16[2,8,2,7,8,8,128]{6,5,3,2,0,1,4:T(8,128)(2,1)} %bitcast.4) | data formatting | bytes 7340032 | tf_op jit(solution)/shard_map/transpose | solution.py:133
  148.3 12.7 %shard_map.75 = bf16[128,4096]{1,0:T(8,128)(2,1)} custom-call(s32[1]{0:T(128)} %dynamic_slice.6.alive_ref, f32[128,128]{1,0:T(8,128)} %get-tuple-element.9.cos_ref, f32[128,128]{1,0:T(8,128)} %get-tuple-element.10.sin_ref, bf16[128,4096]{1,0:T(8,128)(2,1)} %q_ref.1, bf16[128,1024]{1,0:T(8,128)(2,1)} %get-tuple-element.11.ko_ref, bf16[128,1024]{1,0:T(8,128)(2,1)} %vo_ref.1, ...), custom_call_target="tpu_custom_call" | custom-call | tf_op jit(solution)/shard_map/pallas_call | solution.py:144
  (3 shorter events, 0.0 us)
Async XLA Ops:
  4.4 36.5 %all-to-all-start = ((bf16[256,8,128]{2,1,0:T(8,128)(2,1)}), bf16[256,8,128]{2,1,0:T(8,128)(2,1)S(1)}, u32[]{:S(2)}, u32[]{:S(2)}) async-start(bf16[256,8,128]{2,1,0:T(8,128)(2,1)} %bitcast.11), calls=%async_computation | async-start | bytes 1048576 | tf_op jit(solution)/shard_map/all_to_all | solution.py:122
  40.9 0.8 copy-start
  47.9 95.5 %all-to-all-start.1 = ((bf16[256,56,128]{2,1,0:T(8,128)(2,1)}), bf16[256,56,128]{2,1,0:T(8,128)(2,1)}, u32[]{:S(2)}, u32[]{:S(2)}) async-start(bf16[256,56,128]{2,1,0:T(8,128)(2,1)} %bitcast.10), calls=%async_computation.1 | async-start | bytes 7340032 | tf_op jit(solution)/shard_map/all_to_all | solution.py:130
